TPU v7x, 32 devices: a whole 2x2x4 slice. The times are simulated.
32 devices in a mesh: ctx: 16 (over z, x, core), ch: 2 (over y).
Axes of the slice: x: 2, y: 2, z: 4, core: 2. Of those that a mesh axis runs over, the one named last changes fastest.
Arguments:
- q_proj: bfloat16 [512, 16384], P('ch', 'ctx'), may hold values from -6 to 6
- k_proj: bfloat16 [512, 16384], P('ch', 'ctx'), may hold values from -6 to 6
- v_proj: bfloat16 [512, 16384], P('ch', 'ctx'), may hold values from -6 to 6
- short_taps: bfloat16 [3, 512, 3], P(None, 'ch'), may hold values from -3.5 to 3.5
- long_filter: float32 [512, 16384], P('ch', 'ctx'), may hold values from -4 to 4
- skip_gain: float32 [512], P('ch'), may hold values from 0.5 to 1.5
- out_weight: bfloat16 [512, 4096], P(None, 'ch'), may hold values from -0.25 to 0.25
Outputs:
- block_out: bfloat16 [16384, 4096], P('ctx', 'ch')
All inputs are finite; a program needn't handle non-finite values.
Results may differ from a plain program's by a relative error of at most 0.012.
Values may be sent and summed in bfloat16 or wider, within the bound.
No kernel may reach another device: no remote copies, remote signals or barrier semaphores. Data moves between devices by JAX's collectives and lax.ppermute only.
A program may use at most 128 MiB of HBM per device.

v0:
```python
import math
import jax
import jax.numpy as jnp
from jax import lax
from jax.sharding import PartitionSpec as P

exact_mode = lax.Precision.HIGHEST


def passed_along(value, axis, steps):
    count = lax.axis_size(axis)
    initial, last = (max(0, -steps), min(count, count - steps))
    return lax.ppermute(value, axis, [(source, source + steps) for source in range(initial, last)])


def unit_table(numbers, modulus, direction):
    angle = (numbers % modulus).astype(jnp.float32) * (direction * 2.0 * math.pi / modulus)
    return (jnp.cos(angle), jnp.sin(angle))


def complex_contract(pattern, left_real, left_imag, right_real, right_imag):
    real_real = jnp.einsum(pattern, left_real, right_real, precision=exact_mode)
    imag_imag = jnp.einsum(pattern, left_imag, right_imag, precision=exact_mode)
    real_imag = jnp.einsum(pattern, left_real, right_imag, precision=exact_mode)
    imag_real = jnp.einsum(pattern, left_imag, right_real, precision=exact_mode)
    return (real_real - imag_imag, real_imag + imag_real)


def transform_last(real_part, imag_part, inverse):
    size_n = real_part.shape[-1]
    direction = 1.0 if inverse else -1.0
    factor = max([divisor for divisor in range(1, 129) if size_n % divisor == 0])
    if size_n <= 128 or factor == 1:
        counter = jnp.arange(size_n, dtype=jnp.int32)
        table_cos, table_sin = unit_table(counter[:, None] * counter[None, :], size_n, direction)
        return complex_contract("...a,ak->...k", real_part, imag_part, table_cos, table_sin)
    remain = size_n // factor
    leading = real_part.shape[:-1]
    outer = jnp.arange(factor, dtype=jnp.int32)
    inner = jnp.arange(remain, dtype=jnp.int32)
    table_cos, table_sin = unit_table(outer[:, None] * outer[None, :], factor, direction)
    section_real, section_imag = complex_contract(
        "...ab,ac->...cb",
        real_part.reshape(leading + (factor, remain)),
        imag_part.reshape(leading + (factor, remain)),
        table_cos,
        table_sin,
    )
    twist_cos, twist_sin = unit_table(outer[:, None] * inner[None, :], size_n, direction)
    section_real, section_imag = (
        section_real * twist_cos - section_imag * twist_sin,
        section_real * twist_sin + section_imag * twist_cos,
    )
    section_real, section_imag = transform_last(section_real, section_imag, inverse)
    return (
        jnp.swapaxes(section_real, -1, -2).reshape(leading + (size_n,)),
        jnp.swapaxes(section_imag, -1, -2).reshape(leading + (size_n,)),
    )


def short_filter(extended, weights, out_length):
    span = weights.shape[-1]
    summed = jnp.zeros(extended.shape[:-1] + (out_length,), jnp.float32)
    for offset in range(span):
        begin_at = span - 1 - offset
        summed = summed + weights[..., offset : offset + 1].astype(jnp.float32) * extended[
            ..., begin_at : begin_at + out_length
        ].astype(jnp.float32)
    return summed


def long_by_channel(signal, long_filter):
    moved_signal, moved_filter = (
        lax.all_to_all(signal, "ctx", split_axis=0, concat_axis=1, tiled=True),
        lax.all_to_all(long_filter, "ctx", split_axis=0, concat_axis=1, tiled=True),
    )
    seq_len = moved_signal.shape[1]
    both = jnp.stack([moved_signal, moved_filter])
    padded = jnp.concatenate([both, jnp.zeros_like(both)], axis=2)
    freq_real, freq_imag = transform_last(padded, jnp.zeros_like(padded), False)
    prod_real = freq_real[0] * freq_real[1] - freq_imag[0] * freq_imag[1]
    prod_imag = freq_real[0] * freq_imag[1] + freq_imag[0] * freq_real[1]
    time_real, time_imag = transform_last(prod_real, prod_imag, True)
    result_rows = time_real[:, :seq_len] * (1.0 / (2 * seq_len))
    return lax.all_to_all(result_rows, "ctx", split_axis=1, concat_axis=0, tiled=True)


def local(q_proj, k_proj, v_proj, short_taps, long_filter, skip_gain, out_weight):
    channels, tokens = q_proj.shape
    short_span = short_taps.shape[2]
    stacked = jnp.stack([q_proj, k_proj, v_proj])
    rim_short = passed_along(stacked[:, :, tokens - short_span + 1 :], "ctx", 1)
    filtered = short_filter(jnp.concatenate([rim_short, stacked], axis=2), short_taps, tokens)
    query_short = filtered[0]
    product_kv = (filtered[1] * filtered[2]).astype(jnp.bfloat16).astype(jnp.float32)
    long_out = long_by_channel(product_kv, long_filter)
    gated_rows = (query_short * (long_out + skip_gain[:, None] * product_kv)).astype(jnp.bfloat16)
    initial = jnp.zeros((tokens, out_weight.shape[1]), jnp.float32)
    piece = jax.tree.map(lambda part: lax.all_gather(part, "ch", axis=0, tiled=True), gated_rows)
    weight_rows = lax.slice_in_dim(out_weight, 0, piece.shape[0], axis=0)
    summed = initial + jnp.einsum(
        "cb,cd->bd", piece, weight_rows, preferred_element_type=jnp.float32
    )
    return summed.astype(jnp.bfloat16)


def solution(mesh):
    in_specs = (
        P("ch", "ctx"),
        P("ch", "ctx"),
        P("ch", "ctx"),
        P(None, "ch", None),
        P("ch", "ctx"),
        P("ch"),
        P(None, "ch"),
    )
    out_specs = P("ctx", "ch")
    return jax.shard_map(local, mesh=mesh, in_specs=in_specs, out_specs=out_specs, check_vma=False)
```

profile of v0, /device:TPU:0, one launch (start us, length us, event | category | flops | bytes accessed | tf_op | source)
XLA Modules:
  0.0 414.4 jit_solution(9834079985797515446)
XLA Ops:
  6.5 7.7 %all-to-all-start.1 = ((f32[16,16,1024]{2,1,0:T(8,128)}), f32[16,16,1024]{2,1,0:T(8,128)}, u32[]{:S(2)}, u32[]{:S(2)}) async-start(f32[16,16,1024]{2,1,0:T(8,128)} %bitcast.218), calls=%async_computation.1 | async-start | bytes 2097152 | tf_op jit(solution)/shard_map/all_to_all | solution.py:75
  25.2 12.0 %all-to-all-done.1 = f32[16,16,1024]{2,1,0:T(8,128)} async-done(((f32[16,16,1024]{2,1,0:T(8,128)}), f32[16,16,1024]{2,1,0:T(8,128)}, u32[]{:S(2)}, u32[]{:S(2)}) %all-to-all-start.1) | async-done | bytes 1048608 | tf_op jit(solution)/shard_map/all_to_all | solution.py:75
  37.2 14.4 %all-to-all-start = ((f32[16,16,1024]{2,1,0:T(8,128)}), f32[16,16,1024]{2,1,0:T(8,128)S(1)}, u32[]{:S(2)}, u32[]{:S(2)}) async-start(f32[16,16,1024]{2,1,0:T(8,128)} %bitcast.11), calls=%async_computation | async-start | bytes 2097152 | tf_op jit(solution)/shard_map/all_to_all | solution.py:74
  66.9 7.6 %all-to-all-done = f32[16,16,1024]{2,1,0:T(8,128)S(1)} async-done(((f32[16,16,1024]{2,1,0:T(8,128)}), f32[16,16,1024]{2,1,0:T(8,128)S(1)}, u32[]{:S(2)}, u32[]{:S(2)}) %all-to-all-start) | async-done | bytes 1048608 | tf_op jit(solution)/shard_map/all_to_all | solution.py:74
  85.9 9.3 %add_bitcast_fusion.2 = (f32[2,16,128,256]{3,2,1,0:T(8,128)}, f32[2,16,128,256]{3,2,1,0:T(8,128)}) fusion(f32[128,2,16,256]{3,0,2,1:T(8,128)S(1)} %fusion.4, f32[128,256]{1,0:T(8,128)S(1)} %get-tuple-element.20, f32[128,256]{1,0:T(8,128)S(1)} %get-tuple-element.21, f32[128,2,16,256]{3,0,2,1:T(8,128)S(1)} %copy-done.11, f32[2,16,128,256]{3,2,1,0:T(8,128)S(1)} %bitcast.196), kind=kOutput, calls=%fused_computation.10 | convolution fusion | flops 1618182144 | bytes 21233664 | tf_op jit(solution)/shard_map/...ab,ac->...cb/dot_general | solution.py:24
  106.1 8.2 %fusion.37 = f32[128,2,16,128,2]{3,0,4,2,1:T(8,128)} fusion(f32[2,16,128,128,2]{3,2,4,1,0:T(8,128)} %copy.76), kind=kOutput, calls=%fused_computation.75 | convolution fusion | flops 1610842112 | bytes 8388608 | tf_op jit(solution)/shard_map/...ab,ac->...cb/dot_general | solution.py:24
  114.3 5.7 %fusion.35 = f32[128,2,16,128,2]{3,0,4,2,1:T(8,128)} fusion(f32[2,16,128,128,2]{3,2,4,1,0:T(8,128)S(1)} %copy-done.3), kind=kOutput, calls=%fused_computation.73 | convolution fusion | flops 1610842112 | bytes 8388608 | tf_op jit(solution)/shard_map/...ab,ac->...cb/dot_general | solution.py:22
  119.9 5.7 %copy.77 = f32[2,16,128,256]{2,1,3,0:T(8,128)} copy(f32[2,16,128,256]{3,2,1,0:T(8,128)} %get-tuple-element.5) | data formatting | bytes 8388608 | tf_op jit(solution)/shard_map/add | solution.py:52
  130.9 7.8 %convolution_add_fusion = f32[128,2,16,128,2]{3,0,4,2,1:T(8,128)S(1)} fusion(f32[128,2,16,128,2]{3,0,4,2,1:T(8,128)} %fusion.37, f32[2,16,128,128,2]{3,2,4,1,0:T(8,128)} %copy.78), kind=kOutput, calls=%fused_computation.16 | convolution fusion | flops 1611890688 | bytes 12582912 | tf_op jit(solution)/shard_map/...ab,ac->...cb/dot_general | solution.py:25
  138.7 7.6 %add_bitcast_fusion.1 = (f32[2,16,128,128,2]{2,3,4,1,0:T(8,128)}, f32[2,16,128,128,2]{2,3,4,1,0:T(8,128)}) fusion(f32[128,2,16,128,2]{3,0,4,2,1:T(8,128)S(1)} %convolution_add_fusion, f32[128,2]{0,1:T(2,128)S(1)} %get-tuple-element.22, f32[128,2]{0,1:T(2,128)S(1)} %get-tuple-element.23, f32[128,2,16,128,2]{3,0,4,2,1:T(8,128)S(1)} %copy-done.12, ...), kind=kOutput, calls=%fused_computation.8 | convolution fusion | flops 1618182144 | bytes 20973568 | tf_op jit(solution)/shard_map/...ab,ac->...cb/dot_general | solution.py:23
  146.3 7.2 %copy.81 = f32[2,16,128,128,2]{3,4,2,1,0:T(2,128)} copy(f32[2,16,128,128,2]{2,3,4,1,0:T(8,128)} %get-tuple-element.8) | data formatting | bytes 8388608 | tf_op jit(solution)/shard_map/sub | solution.py:51
  153.5 18.1 %fusion.90 = f32[2,16,128,128,2]{3,4,2,1,0:T(2,128)} fusion(f32[2,16,128,128,2]{3,4,2,1,0:T(2,128)} %copy.81), kind=kOutput, calls=%fused_computation.128 | convolution fusion | flops 25165880 | bytes 8388608 | tf_op jit(solution)/shard_map/...a,ak->...k/dot_general | solution.py:22
  171.6 16.2 %fusion.92 = f32[2,16,128,128,2]{3,4,2,1,0:T(2,128)} fusion(f32[2,16,128,128,2]{3,4,2,1,0:T(2,128)S(1)} %copy-done.1), kind=kOutput, calls=%fused_computation.130 | convolution fusion | flops 25165880 | bytes 8388608 | tf_op jit(solution)/shard_map/...a,ak->...k/dot_general | solution.py:24
  187.8 7.2 %copy.82 = f32[2,16,128,128,2]{3,4,2,1,0:T(2,128)} copy(f32[2,16,128,128,2]{2,3,4,1,0:T(8,128)} %get-tuple-element.7) | data formatting | bytes 8388608 | tf_op jit(solution)/shard_map/add | solution.py:52
  195.1 18.5 %subtract_bitcast_fusion = f32[2,16,128,2,128]{4,3,2,1,0:T(2,128)} fusion(f32[2,16,128,128,2]{3,4,2,1,0:T(2,128)} %fusion.90, f32[2,16,128,128,2]{3,4,2,1,0:T(2,128)} %copy.82), kind=kOutput, calls=%fused_computation.7 | convolution fusion | flops 26214456 | bytes 12582912 | tf_op jit(solution)/shard_map/...a,ak->...k/dot_general | solution.py:23
  213.6 6.4 %reshape.226 = f32[2,16,128,256]{3,2,1,0:T(8,128)} reshape(f32[2,16,128,2,128]{4,3,2,1,0:T(2,128)} %subtract_bitcast_fusion) | data formatting | bytes 8388608 | tf_op jit(solution)/shard_map/reshape | solution.py:56
  220.0 18.4 %add_bitcast_fusion = f32[2,16,128,2,128]{4,3,2,1,0:T(2,128)} fusion(f32[2,16,128,128,2]{3,4,2,1,0:T(2,128)} %fusion.92, f32[2,16,128,128,2]{3,4,2,1,0:T(2,128)} %copy.82), kind=kOutput, calls=%fused_computation.6 | convolution fusion | flops 26214456 | bytes 12582912 | tf_op jit(solution)/shard_map/...a,ak->...k/dot_general | solution.py:25
  238.4 6.7 %reshape.227 = f32[2,16,128,256]{3,2,1,0:T(8,128)} reshape(f32[2,16,128,2,128]{4,3,2,1,0:T(2,128)} %add_bitcast_fusion) | data formatting | bytes 8388608 | tf_op jit(solution)/shard_map/reshape | solution.py:57
  245.1 6.5 %multiply_add_fusion.1 = (f32[1,16,256,128]{2,3,1,0:T(8,128)}, f32[1,16,256,128]{2,3,1,0:T(8,128)}) fusion(f32[2,16,256,128]{2,3,1,0:T(8,128)} %bitcast.198, f32[2,16,256,128]{2,3,1,0:T(8,128)} %bitcast.197), kind=kLoop, calls=%fused_computation.24 | loop fusion | flops 3145728 | bytes 12582912 | tf_op jit(solution)/shard_map/add | solution.py:82
  315.8 9.9 %fusion.87 = f32[16,128,128,2]{2,3,1,0:T(2,128)} fusion(f32[16,128,128,2]{2,3,1,0:T(2,128)} %copy.93), kind=kOutput, calls=%fused_computation.125 | convolution fusion | flops 12582968 | bytes 4194304 | tf_op jit(solution)/shard_map/...a,ak->...k/dot_general | solution.py:22
  329.8 10.2 %subtract_bitcast_fusion.3 = f32[16,128,2,128]{3,2,1,0:T(2,128)} fusion(f32[16,128,128,2]{2,3,1,0:T(2,128)} %fusion.87, f32[16,128,128,2]{2,3,1,0:T(2,128)} %copy.94), kind=kOutput, calls=%fused_computation.19 | convolution fusion | flops 13107256 | bytes 6291456 | tf_op jit(solution)/shard_map/...a,ak->...k/dot_general | solution.py:23
  347.2 31.6 %all_to_all.48 = f32[16,16,1024]{2,0,1:T(8,128)S(1)} all-to-all(f32[16,16,1024]{2,0,1:T(8,128)S(1)} %bitcast.217), channel_id=1, replica_groups=mesh['ctx'=16,'ch'=2] {'ctx'}, dimensions={1} | all-to-all | bytes 2097152 | tf_op jit(solution)/shard_map/all_to_all | solution.py:85
  379.8 21.8 %all-gather.2.cloned.1.call-done = bf16[512,1024]{1,0:T(8,128)(2,1)} async-done(((bf16[256,1024]{1,0:T(8,128)(2,1)}), bf16[512,1024]{1,0:T(8,128)(2,1)}) %all-gather.2.cloned.1.call-update) | async-done | bytes 1048592 | tf_op jit(solution)/shard_map/all_gather | solution.py:99
  401.7 5.6 %convolution_convert_fusion = bf16[1024,2048]{1,0:T(8,128)(2,1)} fusion(bf16[512,1024]{1,0:T(8,128)(2,1)} %all-gather.2.cloned.1.call-done, bf16[512,2048]{1,0:T(8,128)(2,1)S(1)} %copy-done), kind=kOutput, calls=%fused_computation.12 | convolution fusion | flops 2149580800 | bytes 7340032 | tf_op jit(solution)/shard_map/cb,cd->bd/dot_general | solution.py:101
  (93 shorter events, 130.0 us)
Async XLA Ops:
  6.5 395.1 %copy-start = (bf16[512,2048]{1,0:T(8,128)(2,1)S(1)}, bf16[512,2048]{1,0:T(8,128)(2,1)}, u32[]{:S(2)}) copy-start(bf16[512,2048]{1,0:T(8,128)(2,1)} %param.13) | copy-start | bytes 6291460
  6.5 12.8 %copy-start.16 = (bf16[256,1024]{1,0:T(8,128)(2,1)S(1)}, bf16[256,1024]{1,0:T(8,128)(2,1)}, u32[]{:S(2)}) copy-start(bf16[256,1024]{1,0:T(8,128)(2,1)} %param.8) | copy-start | bytes 1572868
  6.5 12.8 %copy-start.15 = (bf16[256,1024]{1,0:T(8,128)(2,1)S(1)}, bf16[256,1024]{1,0:T(8,128)(2,1)}, u32[]{:S(2)}) copy-start(bf16[256,1024]{1,0:T(8,128)(2,1)} %param.9) | copy-start | bytes 1572868
  6.5 11.7 %copy-start.19 = (bf16[3,256,3]{1,2,0:T(4,128)(2,1)S(1)}, bf16[3,256,3]{1,2,0:T(4,128)(2,1)}, u32[]{:S(2)}) copy-start(bf16[3,256,3]{1,2,0:T(4,128)(2,1)} %param.10) | copy-start | bytes 13828
  6.5 30.7 %all-to-all-start.1 = ((f32[16,16,1024]{2,1,0:T(8,128)}), f32[16,16,1024]{2,1,0:T(8,128)}, u32[]{:S(2)}, u32[]{:S(2)}) async-start(f32[16,16,1024]{2,1,0:T(8,128)} %bitcast.218), calls=%async_computation.1 | async-start | bytes 2097152 | tf_op jit(solution)/shard_map/all_to_all | solution.py:75
  14.3 5.1 %copy-start.17 = (bf16[256,1024]{1,0:T(8,128)(2,1)S(1)}, bf16[256,1024]{1,0:T(8,128)(2,1)}, u32[]{:S(2)}) copy-start(bf16[256,1024]{1,0:T(8,128)(2,1)} %param.7) | copy-start | bytes 1572868
  16.0 3.3 collective-permute-start
  37.2 37.3 %all-to-all-start = ((f32[16,16,1024]{2,1,0:T(8,128)}), f32[16,16,1024]{2,1,0:T(8,128)S(1)}, u32[]{:S(2)}, u32[]{:S(2)}) async-start(f32[16,16,1024]{2,1,0:T(8,128)} %bitcast.11), calls=%async_computation | async-start | bytes 2097152 | tf_op jit(solution)/shard_map/all_to_all | solution.py:74
  51.6 350.1 %all-gather.2.cloned.1.call-start = ((), (), s32[]{:S(2)}) async-start(), calls=%async_computation.3 | async-start | bytes 1572864 | tf_op jit(solution)/shard_map/all_gather | solution.py:99
  79.0 2.2 copy-start.10
  81.2 4.7 %copy-start.11 = (f32[128,2,16,256]{3,0,2,1:T(8,128)S(1)}, f32[128,2,16,256]{3,0,2,1:T(8,128)}, u32[]{:S(2)}) copy-start(f32[128,2,16,256]{3,0,2,1:T(8,128)} %fusion.10) | copy-start | bytes 12582916
  106.1 8.2 %copy-start.3 = (f32[2,16,128,128,2]{3,2,4,1,0:T(8,128)S(1)}, f32[2,16,128,128,2]{3,2,4,1,0:T(8,128)}, u32[]{:S(2)}) copy-start(f32[2,16,128,128,2]{3,2,4,1,0:T(8,128)} %copy.76) | copy-start | bytes 12582916
  130.9 7.8 %copy-start.2 = (f32[2,16,128,128,2]{3,2,4,1,0:T(8,128)S(1)}, f32[2,16,128,128,2]{3,2,4,1,0:T(8,128)}, u32[]{:S(2)}) copy-start(f32[2,16,128,128,2]{3,2,4,1,0:T(8,128)} %copy.78) | copy-start | bytes 12582916
  130.9 7.8 %copy-start.12 = (f32[128,2,16,128,2]{3,0,4,2,1:T(8,128)S(1)}, f32[128,2,16,128,2]{3,0,4,2,1:T(8,128)}, u32[]{:S(2)}) copy-start(f32[128,2,16,128,2]{3,0,4,2,1:T(8,128)} %fusion.35) | copy-start | bytes 12582916
  153.5 18.1 %copy-start.1 = (f32[2,16,128,128,2]{3,4,2,1,0:T(2,128)S(1)}, f32[2,16,128,128,2]{3,4,2,1,0:T(2,128)}, u32[]{:S(2)}) copy-start(f32[2,16,128,128,2]{3,4,2,1,0:T(2,128)} %copy.81) | copy-start | bytes 12582916
  257.4 5.2 %copy-start.8 = (f32[16,128,256]{2,1,0:T(8,128)S(1)}, f32[16,128,256]{2,1,0:T(8,128)}, u32[]{:S(2)}) copy-start(f32[16,128,256]{2,1,0:T(8,128)} %sub.70) | copy-start | bytes 6291460
  271.9 4.6 %copy-start.6 = (f32[16,128,256]{2,1,0:T(8,128)S(1)}, f32[16,128,256]{2,1,0:T(8,128)}, u32[]{:S(2)}) copy-start(f32[16,128,256]{2,1,0:T(8,128)} %add.212) | copy-start | bytes 6291460
  271.9 4.6 %copy-start.13 = (f32[128,16,256]{2,0,1:T(8,128)S(1)}, f32[128,16,256]{2,0,1:T(8,128)}, u32[]{:S(2)}) copy-start(f32[128,16,256]{2,0,1:T(8,128)} %fusion.45) | copy-start | bytes 6291460
  271.9 4.6 %copy-start.18 = (f32[128,256]{1,0:T(8,128)S(1)}, f32[128,256]{1,0:T(8,128)}, u32[]{:S(2)}) copy-start(f32[128,256]{1,0:T(8,128)} %get-tuple-element.25) | copy-start | bytes 393220
  287.7 5.2 %copy-start.9 = (f32[16,128,128,2]{2,1,3,0:T(8,128)S(1)}, f32[16,128,128,2]{2,1,3,0:T(8,128)}, u32[]{:S(2)}) copy-start(f32[16,128,128,2]{2,1,3,0:T(8,128)} %copy.88) | copy-start | bytes 6291460
  302.3 4.5 %copy-start.7 = (f32[16,128,128,2]{2,1,3,0:T(8,128)S(1)}, f32[16,128,128,2]{2,1,3,0:T(8,128)}, u32[]{:S(2)}) copy-start(f32[16,128,128,2]{2,1,3,0:T(8,128)} %copy.90) | copy-start | bytes 6291460
  302.3 4.6 %copy-start.14 = (f32[128,16,128,2]{2,0,3,1:T(8,128)S(1)}, f32[128,16,128,2]{2,0,3,1:T(8,128)}, u32[]{:S(2)}) copy-start(f32[128,16,128,2]{2,0,3,1:T(8,128)} %fusion.26) | copy-start | bytes 6291460
  346.9 31.8 %copy-start.5 = (f32[3,256,1024]{2,1,0:T(8,128)S(1)}, f32[3,256,1024]{2,1,0:T(8,128)}, u32[]{:S(2)}) copy-start(f32[3,256,1024]{2,1,0:T(8,128)} %copy-done.4) | copy-start | bytes 9437188
  347.0 31.8 %copy-start.20 = (f32[256]{0:T(256)S(1)}, f32[256]{0:T(256)}, u32[]{:S(2)}) copy-start(f32[256]{0:T(256)} %param.12) | copy-start | bytes 3076
  (1 other events, 1.6 us)
Sparse Core Ops, SparseCore 0:
  380.0 21.6 all-gather.1
where the time goes:
time: 419 us; the launch traced here: 414 us
  matrix products  184 us (44%)
  local copies, waits for them, and re-layouts  101 us (24%)
  waiting for transfers between devices  42.5 us (10%)
  blocking collectives  31.6 us (8%)
  starting transfers between devices  25 us (6%)
  other arithmetic  16.7 us (4%)
  between operations  13.9 us (3%)
    dot_general x6, matrix products, complex_contract(): imag_imag = jnp.einsum(pattern, left_imag, right_imag, precision=exact_mode)  49.7 us
    dot_general x6, matrix products, complex_contract(): real_real = jnp.einsum(pattern, left_real, right_real, precision=exact_mode)  45.3 us
    dot_general x5, matrix products, complex_contract(): real_imag = jnp.einsum(pattern, left_real, right_imag, precision=exact_mode)  44.1 us
    dot_general x5, matrix products, complex_contract(): imag_real = jnp.einsum(pattern, left_imag, right_real, precision=exact_mode)  39.1 us
    all_to_all x1, blocking collectives, long_by_channel(): lax.all_to_all(result_rows, 'ctx', split_axis=1, concat_axis=0, tiled=True)  31.6 us
    all_gather x1, waiting for transfers between devices, local(): lax.all_gather(part, 'ch', axis=0, tiled=True)  21.8 us
    add x4, local copies, waits for them, and re-layouts, transform_last(): section_real * twist_sin + section_imag * twist_cos  20.1 us
    sub x4, local copies, waits for them, and re-layouts, transform_last(): section_real * twist_cos - section_imag * twist_sin  19.8 us
  transfers between devices with their start and end apart: 4, of which 4 were waited for; matrix products, arithmetic and copies ran while one was open for 5% of the time, Pallas kernels for 0%

commit v1 on v0

--- a/solution.py
+++ b/solution.py
@@ -5,6 +5,29 @@
 from jax.sharding import PartitionSpec as P
 
 exact_mode = lax.Precision.HIGHEST
+
+
+def apply_the_rounds(incoming_x, dim_at):
+    long_array = list(incoming_x.shape[1:])
+    long_array[dim_at] *= incoming_x.shape[0]
+    raw_out = jnp.moveaxis(incoming_x, 0, dim_at).reshape(long_array)
+    return raw_out
+
+
+def set_the_bars(packet, named_axis):
+    state_now = lax.axis_size(named_axis)
+    frame_out = lax.axis_index(named_axis)
+    local_part, y = (state_now, frame_out)
+    current_arr, current_value = (packet[None], 1)
+    while current_value < local_part:
+        arr_now = tuple(((it, it ^ current_value) for it in range(local_part)))
+        block_last = lax.ppermute(current_arr, named_axis, arr_now)
+        val = y & current_value == 0
+        opened = jnp.where(val, current_arr, block_last)
+        top = jnp.where(val, block_last, current_arr)
+        current_arr = jnp.concatenate([opened, top])
+        current_value *= 2
+    return current_arr
 
 
 def passed_along(value, axis, steps):
@@ -96,7 +119,13 @@
     long_out = long_by_channel(product_kv, long_filter)
     gated_rows = (query_short * (long_out + skip_gain[:, None] * product_kv)).astype(jnp.bfloat16)
     initial = jnp.zeros((tokens, out_weight.shape[1]), jnp.float32)
-    piece = jax.tree.map(lambda part: lax.all_gather(part, "ch", axis=0, tiled=True), gated_rows)
+
+    def review_matrix(local_block, own_rows, dim_no):
+        before = set_the_bars(local_block, own_rows)
+        res = apply_the_rounds(before, dim_no)
+        return res
+
+    piece = jax.tree.map(lambda part: review_matrix(part, "ch", 0), gated_rows)
     weight_rows = lax.slice_in_dim(out_weight, 0, piece.shape[0], axis=0)
     summed = initial + jnp.einsum(
         "cb,cd->bd", piece, weight_rows, preferred_element_type=jnp.float32

time: 419 us -> 397 us (0.947)
  between operations: 13.9 us -> 0.54 us
  waiting for transfers between devices: 42.5 us -> 34.5 us
    all_gather x1 -> x0, waiting for transfers between devices: 21.8 us -> none  [local(): lax.all_gather(part, 'ch', axis=0, tiled=True)]
    ppermute x0 -> x1, waiting for transfers between devices: none -> 13.3 us  [set_the_bars(): block_last = lax.ppermute(current_arr, named_axis, arr_now)]
where the time goes in v1:
time: 397 us; the launch traced here: 393 us
  matrix products  182 us (46%)
  local copies, waits for them, and re-layouts  101 us (25%)
  waiting for transfers between devices  34.5 us (9%)
  blocking collectives  31.6 us (8%)
  starting transfers between devices  26.6 us (7%)
  other arithmetic  16.1 us (4%)
    dot_general x6, matrix products, complex_contract(): imag_imag = jnp.einsum(pattern, left_imag, right_imag, precision=exact_mode)  49.7 us
    dot_general x6, matrix products, complex_contract(): real_real = jnp.einsum(pattern, left_real, right_real, precision=exact_mode)  45.3 us
    dot_general x5, matrix products, complex_contract(): real_imag = jnp.einsum(pattern, left_real, right_imag, precision=exact_mode)  44.1 us
    dot_general x5, matrix products, complex_contract(): imag_real = jnp.einsum(pattern, left_imag, right_real, precision=exact_mode)  39.1 us
    all_to_all x1, blocking collectives, long_by_channel(): lax.all_to_all(result_rows, 'ctx', split_axis=1, concat_axis=0, tiled=True)  31.6 us
    add x4, local copies, waits for them, and re-layouts, transform_last(): section_real * twist_sin + section_imag * twist_cos  20 us
    sub x4, local copies, waits for them, and re-layouts, transform_last(): section_real * twist_cos - section_imag * twist_sin  19.9 us
    all_to_all x1, starting transfers between devices, long_by_channel(): lax.all_to_all(signal, 'ctx', split_axis=0, concat_axis=1, tiled=True)  15 us
  transfers between devices with their start and end apart: 4, of which 4 were waited for; matrix products, arithmetic and copies ran while one was open for 5% of the time, Pallas kernels for 0%

profile of v1, /device:TPU:0, one launch (start us, length us, event | category | flops | bytes accessed | tf_op | source)
XLA Modules:
  0.0 392.7 jit_solution(12104842126940250411)
XLA Ops:
  0.0 7.7 %all-to-all-start.1 = ((f32[16,16,1024]{2,1,0:T(8,128)}), f32[16,16,1024]{2,1,0:T(8,128)}, u32[]{:S(2)}, u32[]{:S(2)}) async-start(f32[16,16,1024]{2,1,0:T(8,128)} %bitcast.209), calls=%async_computation.1 | async-start | bytes 2097152 | tf_op jit(solution)/shard_map/all_to_all | solution.py:98
  18.7 12.0 %all-to-all-done.1 = f32[16,16,1024]{2,1,0:T(8,128)} async-done(((f32[16,16,1024]{2,1,0:T(8,128)}), f32[16,16,1024]{2,1,0:T(8,128)}, u32[]{:S(2)}, u32[]{:S(2)}) %all-to-all-start.1) | async-done | bytes 1048608 | tf_op jit(solution)/shard_map/all_to_all | solution.py:98
  30.7 15.0 %all-to-all-start = ((f32[16,16,1024]{2,1,0:T(8,128)}), f32[16,16,1024]{2,1,0:T(8,128)S(1)}, u32[]{:S(2)}, u32[]{:S(2)}) async-start(f32[16,16,1024]{2,1,0:T(8,128)} %bitcast.10), calls=%async_computation | async-start | bytes 2097152 | tf_op jit(solution)/shard_map/all_to_all | solution.py:97
  60.3 8.3 %all-to-all-done = f32[16,16,1024]{2,1,0:T(8,128)S(1)} async-done(((f32[16,16,1024]{2,1,0:T(8,128)}), f32[16,16,1024]{2,1,0:T(8,128)S(1)}, u32[]{:S(2)}, u32[]{:S(2)}) %all-to-all-start) | async-done | bytes 1048608 | tf_op jit(solution)/shard_map/all_to_all | solution.py:97
  80.0 9.3 %add_bitcast_fusion.2 = (f32[2,16,128,256]{3,2,1,0:T(8,128)}, f32[2,16,128,256]{3,2,1,0:T(8,128)}) fusion(f32[128,2,16,256]{3,0,2,1:T(8,128)S(1)} %fusion.4, f32[128,256]{1,0:T(8,128)S(1)} %get-tuple-element.22, f32[128,256]{1,0:T(8,128)S(1)} %get-tuple-element.23, f32[128,2,16,256]{3,0,2,1:T(8,128)S(1)} %copy-done.11, f32[2,16,128,256]{3,2,1,0:T(8,128)S(1)} %bitcast.187), kind=kOutput, calls=%fused_computation.10 | convolution fusion | flops 1618182144 | bytes 21233664 | tf_op jit(solution)/shard_map/...ab,ac->...cb/dot_general | solution.py:47
  89.2 5.4 %copy.75 = f32[2,16,128,256]{2,1,3,0:T(8,128)} copy(f32[2,16,128,256]{3,2,1,0:T(8,128)} %get-tuple-element.6) | data formatting | bytes 8388608 | tf_op jit(solution)/shard_map/sub | solution.py:74
  100.1 8.2 %fusion.36 = f32[128,2,16,128,2]{3,0,4,2,1:T(8,128)} fusion(f32[2,16,128,128,2]{3,2,4,1,0:T(8,128)} %copy.76), kind=kOutput, calls=%fused_computation.76 | convolution fusion | flops 1610842112 | bytes 8388608 | tf_op jit(solution)/shard_map/...ab,ac->...cb/dot_general | solution.py:47
  108.3 5.6 %fusion.34 = f32[128,2,16,128,2]{3,0,4,2,1:T(8,128)} fusion(f32[2,16,128,128,2]{3,2,4,1,0:T(8,128)S(1)} %copy-done.3), kind=kOutput, calls=%fused_computation.74 | convolution fusion | flops 1610842112 | bytes 8388608 | tf_op jit(solution)/shard_map/...ab,ac->...cb/dot_general | solution.py:45
  113.9 5.7 %copy.77 = f32[2,16,128,256]{2,1,3,0:T(8,128)} copy(f32[2,16,128,256]{3,2,1,0:T(8,128)} %get-tuple-element.5) | data formatting | bytes 8388608 | tf_op jit(solution)/shard_map/add | solution.py:75
  124.9 7.8 %convolution_add_fusion = f32[128,2,16,128,2]{3,0,4,2,1:T(8,128)S(1)} fusion(f32[128,2,16,128,2]{3,0,4,2,1:T(8,128)} %fusion.36, f32[2,16,128,128,2]{3,2,4,1,0:T(8,128)} %copy.78), kind=kOutput, calls=%fused_computation.16 | convolution fusion | flops 1611890688 | bytes 12582912 | tf_op jit(solution)/shard_map/...ab,ac->...cb/dot_general | solution.py:48
  132.7 7.6 %add_bitcast_fusion.1 = (f32[2,16,128,128,2]{2,3,4,1,0:T(8,128)}, f32[2,16,128,128,2]{2,3,4,1,0:T(8,128)}) fusion(f32[128,2,16,128,2]{3,0,4,2,1:T(8,128)S(1)} %convolution_add_fusion, f32[128,2]{0,1:T(2,128)S(1)} %get-tuple-element.24, f32[128,2]{0,1:T(2,128)S(1)} %get-tuple-element.25, f32[128,2,16,128,2]{3,0,4,2,1:T(8,128)S(1)} %copy-done.12, ...), kind=kOutput, calls=%fused_computation.8 | convolution fusion | flops 1618182144 | bytes 20973568 | tf_op jit(solution)/shard_map/...ab,ac->...cb/dot_general | solution.py:46
  140.2 7.2 %copy.81 = f32[2,16,128,128,2]{3,4,2,1,0:T(2,128)} copy(f32[2,16,128,128,2]{2,3,4,1,0:T(8,128)} %get-tuple-element.8) | data formatting | bytes 8388608 | tf_op jit(solution)/shard_map/sub | solution.py:74
  147.5 18.2 %fusion.89 = f32[2,16,128,128,2]{3,4,2,1,0:T(2,128)} fusion(f32[2,16,128,128,2]{3,4,2,1,0:T(2,128)} %copy.81), kind=kOutput, calls=%fused_computation.129 | convolution fusion | flops 25165880 | bytes 8388608 | tf_op jit(solution)/shard_map/...a,ak->...k/dot_general | solution.py:45
  165.7 16.2 %fusion.91 = f32[2,16,128,128,2]{3,4,2,1,0:T(2,128)} fusion(f32[2,16,128,128,2]{3,4,2,1,0:T(2,128)S(1)} %copy-done.1), kind=kOutput, calls=%fused_computation.131 | convolution fusion | flops 25165880 | bytes 8388608 | tf_op jit(solution)/shard_map/...a,ak->...k/dot_general | solution.py:47
  181.9 7.2 %copy.82 = f32[2,16,128,128,2]{3,4,2,1,0:T(2,128)} copy(f32[2,16,128,128,2]{2,3,4,1,0:T(8,128)} %get-tuple-element.7) | data formatting | bytes 8388608 | tf_op jit(solution)/shard_map/add | solution.py:75
  189.1 18.5 %subtract_bitcast_fusion = f32[2,16,128,2,128]{4,3,2,1,0:T(2,128)} fusion(f32[2,16,128,128,2]{3,4,2,1,0:T(2,128)} %fusion.89, f32[2,16,128,128,2]{3,4,2,1,0:T(2,128)} %copy.82), kind=kOutput, calls=%fused_computation.7 | convolution fusion | flops 26214456 | bytes 12582912 | tf_op jit(solution)/shard_map/...a,ak->...k/dot_general | solution.py:46
  207.6 6.4 %reshape.231 = f32[2,16,128,256]{3,2,1,0:T(8,128)} reshape(f32[2,16,128,2,128]{4,3,2,1,0:T(2,128)} %subtract_bitcast_fusion) | data formatting | bytes 8388608 | tf_op jit(solution)/shard_map/reshape | solution.py:79
  214.0 18.4 %add_bitcast_fusion = f32[2,16,128,2,128]{4,3,2,1,0:T(2,128)} fusion(f32[2,16,128,128,2]{3,4,2,1,0:T(2,128)} %fusion.91, f32[2,16,128,128,2]{3,4,2,1,0:T(2,128)} %copy.82), kind=kOutput, calls=%fused_computation.6 | convolution fusion | flops 26214456 | bytes 12582912 | tf_op jit(solution)/shard_map/...a,ak->...k/dot_general | solution.py:48
  232.4 6.7 %reshape.232 = f32[2,16,128,256]{3,2,1,0:T(8,128)} reshape(f32[2,16,128,2,128]{4,3,2,1,0:T(2,128)} %add_bitcast_fusion) | data formatting | bytes 8388608 | tf_op jit(solution)/shard_map/reshape | solution.py:80
  239.1 6.5 %multiply_add_fusion.1 = (f32[1,16,256,128]{2,3,1,0:T(8,128)}, f32[1,16,256,128]{2,3,1,0:T(8,128)}) fusion(f32[2,16,256,128]{2,3,1,0:T(8,128)} %bitcast.189, f32[2,16,256,128]{2,3,1,0:T(8,128)} %bitcast.188), kind=kLoop, calls=%fused_computation.24 | loop fusion | flops 3145728 | bytes 12582912 | tf_op jit(solution)/shard_map/add | solution.py:105
  309.8 9.9 %fusion.86 = f32[16,128,128,2]{2,3,1,0:T(2,128)} fusion(f32[16,128,128,2]{2,3,1,0:T(2,128)} %copy.93), kind=kOutput, calls=%fused_computation.126 | convolution fusion | flops 12582968 | bytes 4194304 | tf_op jit(solution)/shard_map/...a,ak->...k/dot_general | solution.py:45
  323.8 10.2 %subtract_bitcast_fusion.3 = f32[16,128,2,128]{3,2,1,0:T(2,128)} fusion(f32[16,128,128,2]{2,3,1,0:T(2,128)} %fusion.86, f32[16,128,128,2]{2,3,1,0:T(2,128)} %copy.94), kind=kOutput, calls=%fused_computation.19 | convolution fusion | flops 13107256 | bytes 6291456 | tf_op jit(solution)/shard_map/...a,ak->...k/dot_general | solution.py:46
  341.1 31.6 %all_to_all.48 = f32[16,16,1024]{2,0,1:T(8,128)S(1)} all-to-all(f32[16,16,1024]{2,0,1:T(8,128)S(1)} %bitcast.208), channel_id=1, replica_groups=mesh['ctx'=16,'ch'=2] {'ctx'}, dimensions={1} | all-to-all | bytes 2097152 | tf_op jit(solution)/shard_map/all_to_all | solution.py:108
  374.6 13.3 %collective-permute-done.1 = bf16[1,256,1024]{2,1,0:T(8,128)(2,1)S(1)} collective-permute-done((bf16[1,256,1024]{2,1,0:T(8,128)(2,1)S(1)}, bf16[1,256,1024]{2,1,0:T(8,128)(2,1)S(1)}, u32[]{:S(2)}, u32[]{:S(2)}) %collective-permute-start.1) | collective-permute-done | bytes 524320 | tf_op jit(solution)/shard_map/ppermute | solution.py:24
  (94 shorter events, 129.3 us)
Async XLA Ops:
  0.0 388.1 %copy-start = (bf16[512,2048]{1,0:T(8,128)(2,1)S(1)}, bf16[512,2048]{1,0:T(8,128)(2,1)}, u32[]{:S(2)}) copy-start(bf16[512,2048]{1,0:T(8,128)(2,1)} %param.13) | copy-start | bytes 6291460
  0.0 12.8 %copy-start.16 = (bf16[256,1024]{1,0:T(8,128)(2,1)S(1)}, bf16[256,1024]{1,0:T(8,128)(2,1)}, u32[]{:S(2)}) copy-start(bf16[256,1024]{1,0:T(8,128)(2,1)} %param.8) | copy-start | bytes 1572868
  0.0 12.8 %copy-start.15 = (bf16[256,1024]{1,0:T(8,128)(2,1)S(1)}, bf16[256,1024]{1,0:T(8,128)(2,1)}, u32[]{:S(2)}) copy-start(bf16[256,1024]{1,0:T(8,128)(2,1)} %param.9) | copy-start | bytes 1572868
  0.0 11.7 %copy-start.19 = (bf16[3,256,3]{1,2,0:T(4,128)(2,1)S(1)}, bf16[3,256,3]{1,2,0:T(4,128)(2,1)}, u32[]{:S(2)}) copy-start(bf16[3,256,3]{1,2,0:T(4,128)(2,1)} %param.10) | copy-start | bytes 13828
  0.0 30.7 %all-to-all-start.1 = ((f32[16,16,1024]{2,1,0:T(8,128)}), f32[16,16,1024]{2,1,0:T(8,128)}, u32[]{:S(2)}, u32[]{:S(2)}) async-start(f32[16,16,1024]{2,1,0:T(8,128)} %bitcast.209), calls=%async_computation.1 | async-start | bytes 2097152 | tf_op jit(solution)/shard_map/all_to_all | solution.py:98
  7.7 5.1 %copy-start.17 = (bf16[256,1024]{1,0:T(8,128)(2,1)S(1)}, bf16[256,1024]{1,0:T(8,128)(2,1)}, u32[]{:S(2)}) copy-start(bf16[256,1024]{1,0:T(8,128)(2,1)} %param.7) | copy-start | bytes 1572868
  9.5 3.3 collective-permute-start
  30.7 37.9 %all-to-all-start = ((f32[16,16,1024]{2,1,0:T(8,128)}), f32[16,16,1024]{2,1,0:T(8,128)S(1)}, u32[]{:S(2)}, u32[]{:S(2)}) async-start(f32[16,16,1024]{2,1,0:T(8,128)} %bitcast.10), calls=%async_computation | async-start | bytes 2097152 | tf_op jit(solution)/shard_map/all_to_all | solution.py:97
  73.1 2.2 copy-start.10
  75.3 4.7 %copy-start.11 = (f32[128,2,16,256]{3,0,2,1:T(8,128)S(1)}, f32[128,2,16,256]{3,0,2,1:T(8,128)}, u32[]{:S(2)}) copy-start(f32[128,2,16,256]{3,0,2,1:T(8,128)} %fusion.10) | copy-start | bytes 12582916
  100.1 8.2 %copy-start.3 = (f32[2,16,128,128,2]{3,2,4,1,0:T(8,128)S(1)}, f32[2,16,128,128,2]{3,2,4,1,0:T(8,128)}, u32[]{:S(2)}) copy-start(f32[2,16,128,128,2]{3,2,4,1,0:T(8,128)} %copy.76) | copy-start | bytes 12582916
  124.9 7.8 %copy-start.2 = (f32[2,16,128,128,2]{3,2,4,1,0:T(8,128)S(1)}, f32[2,16,128,128,2]{3,2,4,1,0:T(8,128)}, u32[]{:S(2)}) copy-start(f32[2,16,128,128,2]{3,2,4,1,0:T(8,128)} %copy.78) | copy-start | bytes 12582916
  124.9 7.8 %copy-start.12 = (f32[128,2,16,128,2]{3,0,4,2,1:T(8,128)S(1)}, f32[128,2,16,128,2]{3,0,4,2,1:T(8,128)}, u32[]{:S(2)}) copy-start(f32[128,2,16,128,2]{3,0,4,2,1:T(8,128)} %fusion.34) | copy-start | bytes 12582916
  147.5 18.2 %copy-start.1 = (f32[2,16,128,128,2]{3,4,2,1,0:T(2,128)S(1)}, f32[2,16,128,128,2]{3,4,2,1,0:T(2,128)}, u32[]{:S(2)}) copy-start(f32[2,16,128,128,2]{3,4,2,1,0:T(2,128)} %copy.81) | copy-start | bytes 12582916
  251.4 5.2 %copy-start.8 = (f32[16,128,256]{2,1,0:T(8,128)S(1)}, f32[16,128,256]{2,1,0:T(8,128)}, u32[]{:S(2)}) copy-start(f32[16,128,256]{2,1,0:T(8,128)} %sub.70) | copy-start | bytes 6291460
  265.9 4.6 %copy-start.6 = (f32[16,128,256]{2,1,0:T(8,128)S(1)}, f32[16,128,256]{2,1,0:T(8,128)}, u32[]{:S(2)}) copy-start(f32[16,128,256]{2,1,0:T(8,128)} %add.213) | copy-start | bytes 6291460
  265.9 4.6 %copy-start.13 = (f32[128,16,256]{2,0,1:T(8,128)S(1)}, f32[128,16,256]{2,0,1:T(8,128)}, u32[]{:S(2)}) copy-start(f32[128,16,256]{2,0,1:T(8,128)} %fusion.44) | copy-start | bytes 6291460
  265.9 4.6 %copy-start.18 = (f32[128,256]{1,0:T(8,128)S(1)}, f32[128,256]{1,0:T(8,128)}, u32[]{:S(2)}) copy-start(f32[128,256]{1,0:T(8,128)} %get-tuple-element.27) | copy-start | bytes 393220
  281.6 5.2 %copy-start.9 = (f32[16,128,128,2]{2,1,3,0:T(8,128)S(1)}, f32[16,128,128,2]{2,1,3,0:T(8,128)}, u32[]{:S(2)}) copy-start(f32[16,128,128,2]{2,1,3,0:T(8,128)} %copy.88) | copy-start | bytes 6291460
  296.3 4.5 %copy-start.7 = (f32[16,128,128,2]{2,1,3,0:T(8,128)S(1)}, f32[16,128,128,2]{2,1,3,0:T(8,128)}, u32[]{:S(2)}) copy-start(f32[16,128,128,2]{2,1,3,0:T(8,128)} %copy.90) | copy-start | bytes 6291460
  296.3 4.6 %copy-start.14 = (f32[128,16,128,2]{2,0,3,1:T(8,128)S(1)}, f32[128,16,128,2]{2,0,3,1:T(8,128)}, u32[]{:S(2)}) copy-start(f32[128,16,128,2]{2,0,3,1:T(8,128)} %fusion.25) | copy-start | bytes 6291460
  340.9 31.8 %copy-start.5 = (f32[3,256,1024]{2,1,0:T(8,128)S(1)}, f32[3,256,1024]{2,1,0:T(8,128)}, u32[]{:S(2)}) copy-start(f32[3,256,1024]{2,1,0:T(8,128)} %copy-done.4) | copy-start | bytes 9437188
  340.9 31.8 %copy-start.20 = (f32[256]{0:T(256)S(1)}, f32[256]{0:T(256)}, u32[]{:S(2)}) copy-start(f32[256]{0:T(256)} %param.12) | copy-start | bytes 3076
  373.0 14.9 %collective-permute-start.1 = (bf16[1,256,1024]{2,1,0:T(8,128)(2,1)S(1)}, bf16[1,256,1024]{2,1,0:T(8,128)(2,1)S(1)}, u32[]{:S(2)}, u32[]{:S(2)}) collective-permute-start(bf16[1,256,1024]{2,1,0:T(8,128)(2,1)S(1)} %fusion.15), channel_id=1, source_target_pairs={{0,1},{1,0},{2,3},{3,2},{4,5},{5,4},{6,7},{7,6},{8,9},{9,8},{10,11... | collective-permute-start | bytes 1572872 | tf_op jit(solution)/shard_map/ppermute | solution.py:24
  (1 other events, 1.6 us)
